TPU v7x, 128 devices: a whole 4x4x4 slice. The times are simulated.
128 devices in a mesh: dp: 8 (over z_lo, x), expert: 16 (over z_hi, y, core).
Axes of the slice: x: 4, y: 4, z: 4 (z_hi: 2, z_lo: 2; z = z_hi * 2 + z_lo), core: 2. Of those that a mesh axis runs over, the one named last changes fastest.
Arguments:
- tokens: bfloat16 [196608, 2048], P(('dp', 'expert')), may hold values from -6 to 6
- upstream: bfloat16 [196608, 2048], P(('dp', 'expert')), may hold values from -6 to 6
- counts: int32 [2048], P(('dp', 'expert')), may hold values from 1 to 96, 122880 in all
- assign: int32 [2, 16], replicated, may hold values from 0 to 31
- gate_weight: bfloat16 [32, 512, 2048], P(None, 'expert', 'dp'), may hold values from -0.125 to 0.125
- up_weight: bfloat16 [32, 512, 2048], P(None, 'expert', 'dp'), may hold values from -0.125 to 0.125
- down_weight: bfloat16 [32, 512, 2048], P(None, 'expert', 'dp'), may hold values from -0.25 to 0.25
Outputs:
- token_grad: bfloat16 [196608, 2048], P(('dp', 'expert'))
- gate_weight_grad: float32 [32, 512, 2048], P(None, 'expert', 'dp')
- up_weight_grad: float32 [32, 512, 2048], P(None, 'expert', 'dp')
- down_weight_grad: float32 [32, 512, 2048], P(None, 'expert', 'dp')
Inputs may be any that keep to these rules, and one draw needn't show every extreme that they name: assign[s, i] is the expert used by copy slot i in microstep s; several slots may use the same expert. counts[j] live leading rows in micro-batch j of 96 slots; some micro-batch is full in every draw.
All inputs are finite; a program needn't handle non-finite values. No bound on the sum of `counts` on one device may be relied on, other than what follows from the above.
Results may differ from a plain program's by a relative error of at most 0.012.
Values may be sent and summed in bfloat16 or wider, within the bound.
A program may use at most 128 MiB of HBM per device.

v0:
```python
import functools

import jax
import jax.numpy as jnp
from jax import lax
from jax.experimental import pallas as pl
from jax.experimental.pallas import tpu as pltpu
from jax.sharding import PartitionSpec as P

MESH = pl.DeviceIdType.MESH
F32 = jnp.float32
BF16 = jnp.bfloat16
NT = (((1,), (1,)), ((), ()))
NN = (((1,), (0,)), ((), ()))

NA = 9
HA = 5
HB = 3
VMEM_BYTES = 67043328


def fused_kernel(cfg, assign_ref, live_ref, tok_ref, ups_ref, gate_ref, up_ref, down_ref,
                 tg_out, recv_out,
                 stage, wfull, part, rz, rhla, rhlb, rhra, rhrb, rfla, rflb, rfra, rfrb, rza,
                 xg, acc, t3, gn, tg,
                 w_send, w_recv, g_send, g_recv, ag_send, ag_recv, rs_send, rs_recv,
                 xg_sem, tg_sem, own_sem):
    G, NX, steps, block, rows, width, units = cfg
    NB = units - NA
    half = units // 2
    hrows = half * rows
    dp = lax.axis_index("dp")
    g = lax.axis_index("expert")
    x = dp % NX
    z = dp // NX
    zh = g // half
    right = (x + 1) % NX
    left = (x + NX - 1) % NX
    opp = (x + 2) % NX
    zz = 1 - z
    pS, pL, pR, pO = z * NX + x, z * NX + left, z * NX + right, z * NX + opp
    qS, qL, qR, qO = zz * NX + x, zz * NX + left, zz * NX + right, zz * NX + opp
    dev_r = {"dp": pR, "expert": g}
    dev_l = {"dp": pL, "expert": g}
    dev_z = {"dp": qS, "expert": g}

    A = pl.ds(0, NA)
    A1 = pl.ds(0, HA)
    A2 = pl.ds(HA, NA - HA)
    B = pl.ds(NA, NB)
    B1 = pl.ds(NA, HB)
    B2 = pl.ds(NA + HB, NB - HB)

    def peer(j):
        gp = (g + j) % G
        zp = (z + zh + gp // half) % 2
        return gp, {"dp": zp * NX + x, "expert": gp}

    barrier = pltpu.get_barrier_semaphore()

    def greet(j, carry):
        pl.semaphore_signal(barrier, inc=1, device_id=peer(j)[1], device_id_type=MESH)
        return carry

    lax.fori_loop(1, G, greet, 0)
    for dev in (dev_r, dev_l, dev_z):
        pl.semaphore_signal(barrier, inc=1, device_id=dev, device_id_type=MESH)

    def load_xg(s):
        def one(d, carry):
            cols = pl.ds(pl.multiple_of(d * width, width), width)
            for k, ref in enumerate((tok_ref, ups_ref)):
                pltpu.make_async_copy(ref.at[pl.ds(s * block, block), cols], xg.at[k, d], xg_sem.at[s]).start()
            return carry

        lax.fori_loop(0, 2 * NX, one, 0)

    def wait_xg(s):
        pltpu.make_async_copy(xg, xg, xg_sem.at[s]).wait()

    load_xg(0)

    def pick(s):
        def one(i, carry):
            c = assign_ref[s, i]
            stage[s, i, 0] = gate_ref[c]
            stage[s, i, 1] = up_ref[c]
            stage[s, i, 2] = down_ref[c]
            return carry

        lax.fori_loop(0, G, one, 0)
        wfull[s, pS, g] = stage[s, g]

    pick(0)
    pl.semaphore_wait(barrier, G - 1 + 3)

    def spread(s):
        def one(j, carry):
            gp, dev = peer(j)
            pltpu.make_async_remote_copy(
                stage.at[s, gp], wfull.at[s, dev["dp"], g], w_send.at[s], w_recv.at[s],
                device_id=dev, device_id_type=MESH).start()
            return carry

        lax.fori_loop(1, G, one, 0)

    def spread_wait(s):
        few = pl.ds(0, G - 1)
        pltpu.make_async_copy(stage.at[s, few], stage.at[s, few], w_recv.at[s]).wait()

    pending = []

    def send(src, dst, ssem, rsem, dev):
        copy = pltpu.make_async_remote_copy(src, dst, ssem, rsem, device_id=dev, device_id_type=MESH)
        copy.start()
        pending.append(copy)
        return copy

    class Gather:
        def __init__(self, s):
            self.s = s
            self.c = {}

        def go(self, k, p, piece, dev):
            ref = wfull.at[self.s, p, piece]
            self.c[k] = send(ref, ref, ag_send.at[self.s, k], ag_recv.at[self.s, k], dev)

        def first(self):
            spread_wait(self.s)
            self.go(0, pS, B, dev_r)
            self.go(1, pS, B, dev_l)
            self.go(2, pS, A, dev_z)
            self.go(3, pS, A, dev_r)
            self.go(4, pS, A, dev_l)
            self.go(5, pS, B, dev_z)

        def w(self, *ks):
            for k in ks:
                self.c[k].wait_recv()

        def relay_b(self):
            self.w(0)
            self.go(6, pL, B1, dev_r)
            self.go(10, pL, B, dev_z)
            self.w(1)
            self.go(7, pR, B2, dev_l)
            self.go(11, pR, B, dev_z)

        def partner_a(self):
            self.w(2)
            self.go(8, qS, A, dev_r)
            self.go(9, qS, A, dev_l)

        def relay_a(self):
            self.w(3)
            self.go(12, pL, A1, dev_r)
            self.w(4)
            self.go(13, pR, A2, dev_l)

        def opp_b(self):
            self.w(6)
            self.go(16, pO, B1, dev_z)
            self.w(7)
            self.go(17, pO, B2, dev_z)

        def relay_pa(self):
            self.w(8)
            self.go(14, qL, A1, dev_r)
            self.w(9)
            self.go(15, qR, A2, dev_l)

    def add_into(dst, *others):
        total = dst[...].astype(F32)
        for o in others:
            total = total + o[...].astype(F32)
        dst[...] = total.astype(BF16)

    def add_units(n, dst, *others):
        def one(i, carry):
            add_into(dst(i), *[o(i) for o in others])
            return carry

        lax.fori_loop(0, n, one, 0)

    class Reduce:
        def __init__(self, s):
            self.s = s
            self.c = {}

        def go(self, k, src, dst, dev):
            self.c[k] = send(src, dst, rs_send.at[self.s, k], rs_recv.at[self.s, k], dev)

        def w(self, *ks):
            for k in ks:
                self.c[k].wait_recv()

        def first(self):
            s = self.s
            pt = part.at[s]
            self.go(0, pt.at[qO, A1], rhla.at[s, 1], dev_r)
            self.go(1, pt.at[qO, A2], rhra.at[s, 1], dev_l)
            self.go(2, pt.at[qO, B], rz.at[s, 2], dev_z)
            self.go(3, pt.at[pO, A1], rhla.at[s, 0], dev_r)
            self.go(4, pt.at[pO, A2], rhra.at[s, 0], dev_l)

        def first_z(self):
            s = self.s
            pt = part.at[s]
            self.go(5, pt.at[qR, B], rz.at[s, 1], dev_z)
            self.go(6, pt.at[qL, B], rz.at[s, 3], dev_z)
            self.go(7, pt.at[qS, B], rz.at[s, 0], dev_z)

        def mid_q(self):
            s = self.s
            pt = part.at[s]
            self.w(0)
            add_units(HA, lambda i: pt.at[qR, i], lambda i: rhla.at[s, 1, i])
            self.go(8, pt.at[qR, A], rfla.at[s, 1], dev_r)
            self.w(1)
            add_units(NA - HA, lambda i: pt.at[qL, HA + i], lambda i: rhra.at[s, 1, i])
            self.go(9, pt.at[qL, A], rfra.at[s, 1], dev_l)

        def opp_b(self):
            s = self.s
            pt = part.at[s]
            self.w(2)
            add_units(NB, lambda i: pt.at[pO, NA + i], lambda i: rz.at[s, 2, i])
            self.go(10, pt.at[pO, B1], rhlb.at[s], dev_r)
            self.go(11, pt.at[pO, B2], rhrb.at[s], dev_l)

        def mid_p(self):
            s = self.s
            pt = part.at[s]
            self.w(3)
            add_units(HA, lambda i: pt.at[pR, i], lambda i: rhla.at[s, 0, i])
            self.go(12, pt.at[pR, A], rfla.at[s, 0], dev_r)
            self.w(4)
            add_units(NA - HA, lambda i: pt.at[pL, HA + i], lambda i: rhra.at[s, 0, i])
            self.go(13, pt.at[pL, A], rfra.at[s, 0], dev_l)

        def mid_b(self):
            s = self.s
            pt = part.at[s]
            self.w(5, 10)
            add_units(HB, lambda i: pt.at[pR, NA + i], lambda i: rz.at[s, 1, i], lambda i: rhlb.at[s, i])
            add_units(NB - HB, lambda i: pt.at[pR, NA + HB + i], lambda i: rz.at[s, 1, HB + i])
            self.go(14, pt.at[pR, B], rflb.at[s], dev_r)
            self.w(6, 11)
            add_units(HB, lambda i: pt.at[pL, NA + i], lambda i: rz.at[s, 3, i])
            add_units(NB - HB, lambda i: pt.at[pL, NA + HB + i], lambda i: rz.at[s, 3, HB + i], lambda i: rhrb.at[s, i])
            self.go(15, pt.at[pL, B], rfrb.at[s], dev_l)

        def to_partner(self):
            s = self.s
            pt = part.at[s]
            self.w(8, 9)
            add_units(NA, lambda i: pt.at[qS, i], lambda i: rfla.at[s, 1, i], lambda i: rfra.at[s, 1, i])
            self.go(16, pt.at[qS, A], rza.at[s], dev_z)

        def finish(self):
            s = self.s
            pt = part.at[s]
            self.w(7, 14, 15)
            add_units(NB, lambda i: pt.at[pS, NA + i], lambda i: rz.at[s, 0, i], lambda i: rflb.at[s, i], lambda i: rfrb.at[s, i])
            self.w(12, 13, 16)
            add_units(NA, lambda i: pt.at[pS, i], lambda i: rfla.at[s, 0, i], lambda i: rfra.at[s, 0, i], lambda i: rza.at[s, i])

            def one(j, carry):
                gp, dev = peer(j)
                pltpu.make_async_remote_copy(
                    pt.at[pS, gp], recv_out.at[s, g], g_send.at[s], g_recv.at[s],
                    device_id=dev, device_id_type=MESH).start()
                return carry

            lax.fori_loop(1, G, one, 0)
            pltpu.make_async_copy(pt.at[pS, g], recv_out.at[s, g], own_sem.at[s]).start()

        def done(self):
            s = self.s
            few = pl.ds(0, G - 1)
            pltpu.make_async_copy(recv_out.at[s, few], recv_out.at[s, few], g_recv.at[s]).wait()
            pltpu.make_async_copy(part.at[s, pS, 0], recv_out.at[s, 0], own_sem.at[s]).wait()

    def shard_of(p, h):
        return ((p // NX + h + zh) % 2) * NX + p % NX

    def weight(s, p, h, m):
        return wfull[s, p, pl.ds(h * half, half), m].reshape(hrows, width)

    def forward(s, p, start=False):
        def one(j, carry):
            m, h = j // 2, j % 2
            got = lax.dot_general(weight(s, p, h, m), xg[m // 2, shard_of(p, h)], NT, preferred_element_type=F32)
            if start:
                acc[m, h] = got
            else:
                acc[m, h] += got
            return carry

        lax.fori_loop(0, 6, one, 0)

    def gates(s):
        live = live_ref[s] > 0.5
        tall = 32

        def one(j, carry):
            h = j // (hrows // tall)
            at = pl.ds(pl.multiple_of((j % (hrows // tall)) * tall, tall), tall)
            pre = acc[0, h, at, :]
            upv = acc[1, h, at, :]
            hg = jnp.where(live, acc[2, h, at, :], 0.0)
            sig = jax.nn.sigmoid(pre)
            act = pre * sig
            t3[0, h, at, :] = (hg * upv * sig * (1.0 + pre * (1.0 - sig))).astype(BF16)
            t3[1, h, at, :] = (hg * act).astype(BF16)
            t3[2, h, at, :] = jnp.where(live, act * upv, 0.0).astype(BF16)
            return carry

        lax.fori_loop(0, 2 * (hrows // tall), one, 0)

    scale = 1.0 / block

    def parts(s, p):
        def one(j, carry):
            m, h = j // 2, j % 2
            got = lax.dot_general(t3[m, h], xg[m // 2, shard_of(p, h)], NN, preferred_element_type=F32) * scale
            part[s, p, pl.ds(h * half, half), m] = got.astype(BF16).reshape(half, rows, width)
            return carry

        lax.fori_loop(0, 6, one, 0)

    def turn():
        def one(j, carry):
            gn[j // 2, j % 2] = t3[j // 2, j % 2].T
            return carry

        lax.fori_loop(0, 4, one, 0)

    def tg_copy(s, d):
        cols = pl.ds(pl.multiple_of(d * width, width), width)
        return pltpu.make_async_copy(tg.at[d], tg_out.at[pl.ds(s * block, block), cols], tg_sem.at[d])

    def token_grads(s, lo, hi):
        def one(d, carry):
            total = None
            for m in (0, 1):
                for h in (0, 1):
                    got = jnp.dot(gn[m, h], weight(s, shard_of(d, h), h, m), preferred_element_type=F32)
                    total = got if total is None else total + got
            tg[d] = total.astype(BF16)
            tg_copy(s, d).start()
            return carry

        lax.fori_loop(lo, hi, one, 0)

    def tg_wait(s):
        def one(d, carry):
            tg_copy(s, d).wait()
            return carry

        lax.fori_loop(0, 2 * NX, one, 0)

    g0, g1 = Gather(0), Gather(1)
    r0, r1 = Reduce(0), Reduce(1)

    spread(0)
    pick(1)
    g0.first()
    spread(1)
    wait_xg(0)
    forward(0, pS, start=True)
    g0.relay_b()
    g0.partner_a()
    g0.relay_a()
    forward(0, pL)
    forward(0, pR)
    g0.w(5)
    forward(0, qS)
    g0.opp_b()
    g0.relay_pa()
    g1.first()
    g0.w(10)
    forward(0, qL)
    g0.w(11)
    forward(0, qR)
    g0.w(12, 13)
    forward(0, pO)
    g0.w(14, 15, 16, 17)
    forward(0, qO)
    gates(0)
    g1.relay_b()
    g1.partner_a()
    parts(0, qO)
    parts(0, pO)
    parts(0, qR)
    parts(0, qL)
    g1.relay_a()
    parts(0, qS)
    parts(0, pR)
    parts(0, pL)
    parts(0, pS)
    load_xg(1)
    g1.opp_b()
    turn()
    token_grads(0, 0, 4)
    g1.relay_pa()
    r0.first()
    r0.first_z()
    token_grads(0, 4, 8)
    wait_xg(1)
    forward(1, pS, start=True)
    forward(1, pL)
    forward(1, pR)
    g1.w(5)
    forward(1, qS)
    g1.w(10)
    forward(1, qL)
    g1.w(11)
    forward(1, qR)
    g1.w(12, 13)
    forward(1, pO)
    g1.w(14, 15, 16, 17)
    forward(1, qO)
    gates(1)
    r0.mid_q()
    r0.opp_b()
    r0.mid_p()
    parts(1, qO)
    parts(1, pO)
    parts(1, qR)
    parts(1, qL)
    r0.mid_b()
    parts(1, qS)
    parts(1, pR)
    parts(1, pL)
    parts(1, pS)
    r0.to_partner()
    r1.first()
    r1.first_z()
    tg_wait(0)
    turn()
    token_grads(1, 0, 8)
    r0.finish()
    r1.mid_q()
    r1.opp_b()
    r1.mid_p()
    r1.mid_b()
    r1.to_partner()
    r1.finish()
    tg_wait(1)
    r0.done()
    r1.done()
    for copy in pending:
        copy.wait_send()
    for s in range(steps):
        few = pl.ds(0, G - 1)
        pltpu.make_async_copy(stage.at[s, few], stage.at[s, few], w_send.at[s]).wait()
        pltpu.make_async_copy(stage.at[s, few], stage.at[s, few], g_send.at[s]).wait()


def home_kernel(assign_ref, recv_ref, gate_ref, up_ref, down_ref):
    outs = (gate_ref, up_ref, down_ref)
    steps, count = recv_ref.shape[:2]
    for ref in outs:
        ref[...] = jnp.zeros_like(ref)

    def one(i, carry):
        s, k = i // count, i % count
        c = assign_ref[s, k]
        for m, ref in enumerate(outs):
            ref[c] += recv_ref[s, k, m].astype(F32)
        return carry

    lax.fori_loop(0, steps * count, one, 0)


def local(tokens, upstream, counts, assign, gate_weight, up_weight, down_weight):
    steps, G = assign.shape
    batch_count = counts.shape[0] // steps
    block = tokens.shape[0] // steps
    batch_rows = block // batch_count
    experts, rows, width = gate_weight.shape
    dp_count = tokens.shape[1] // width
    NX = dp_count // 2
    position = jnp.arange(batch_rows, dtype=jnp.int32)
    live = (position[None, :] < counts[:, None]).astype(F32).reshape(steps, 1, block)

    NB = G - NA
    unit = (3, rows, width)

    def vm(*shape, dtype=BF16):
        return pltpu.VMEM(shape, dtype)

    dma = pltpu.SemaphoreType.DMA
    half = G // 2
    hrows = half * rows
    scratch = [
        vm(steps, G, *unit),
        vm(steps, dp_count, G, *unit),
        vm(steps, dp_count, G, *unit),
        vm(steps, 4, NB, *unit),
        vm(steps, 2, HA, *unit),
        vm(steps, HB, *unit),
        vm(steps, 2, NA - HA, *unit),
        vm(steps, NB - HB, *unit),
        vm(steps, 2, NA, *unit),
        vm(steps, NB, *unit),
        vm(steps, 2, NA, *unit),
        vm(steps, NB, *unit),
        vm(steps, NA, *unit),
        vm(2, dp_count, block, width),
        vm(3, 2, hrows, block, dtype=F32),
        vm(3, 2, hrows, block),
        vm(2, 2, block, hrows),
        vm(dp_count, block, width),
        dma((steps,)), dma((steps,)), dma((steps,)), dma((steps,)),
        dma((steps, 18)), dma((steps, 18)), dma((steps, 17)), dma((steps, 17)),
        dma((steps,)), dma((dp_count,)), dma((steps,)),
    ]
    vmem = pl.BlockSpec(memory_space=pltpu.VMEM)
    smem = pl.BlockSpec(memory_space=pltpu.SMEM)
    anyw = pl.BlockSpec(memory_space=pl.ANY)
    cfg = (G, NX, steps, block, rows, width, G)
    flops = 2 * steps * 8 * block * (G * rows) * tokens.shape[1]
    token_grad, received = pl.pallas_call(
        functools.partial(fused_kernel, cfg),
        out_shape=(
            jax.ShapeDtypeStruct(tokens.shape, BF16),
            jax.ShapeDtypeStruct((steps, G, *unit), BF16),
        ),
        in_specs=[smem, vmem, anyw, anyw, vmem, vmem, vmem],
        out_specs=(anyw, anyw),
        scratch_shapes=scratch,
        compiler_params=pltpu.CompilerParams(
            collective_id=0, has_side_effects=True, vmem_limit_bytes=VMEM_BYTES
        ),
        cost_estimate=pl.CostEstimate(flops=flops, bytes_accessed=6 * tokens.size, transcendentals=0),
        name="expert_step",
    )(assign, live, tokens, upstream, gate_weight, up_weight, down_weight)

    grad = jax.ShapeDtypeStruct(gate_weight.shape, F32)
    grads = pl.pallas_call(
        home_kernel,
        out_shape=(grad, grad, grad),
        in_specs=[smem, vmem],
        out_specs=(vmem, vmem, vmem),
        name="to_experts",
    )(assign, received)
    return (token_grad, *grads)


def solution(mesh):
    placed = (
        P(("dp", "expert"), None),
        P(("dp", "expert"), None),
        P(("dp", "expert")),
        P(),
        P(None, "expert", "dp"),
        P(None, "expert", "dp"),
        P(None, "expert", "dp"),
    )
    return jax.shard_map(
        local,
        mesh=mesh,
        in_specs=placed,
        out_specs=(
            P(("dp", "expert"), None),
            P(None, "expert", "dp"),
            P(None, "expert", "dp"),
            P(None, "expert", "dp"),
        ),
        check_vma=False,
    )
```

profile of v0, /device:TPU:1, one launch (start us, length us, event | category | flops | bytes accessed | tf_op | source)
XLA Modules:
  0.0 211.7 jit_solution(12543494412662094243)
XLA Ops:
  0.6 0.7 lt.31
  1.4 0.1 lt.29
  1.4 0.1 lt.32
  1.5 0.1 lt.33
  1.6 0.6 compare_convert_fusion.live_ref
  2.2 199.0 %expert_step.1 = (bf16[1536,2048]{1,0:T(8,128)(2,1)}, bf16[2,16,3,32,256]{4,3,2,1,0:T(8,128)(2,1)}) custom-call(s32[2,16]{1,0:T(2,128)} %assign_ref.3, f32[2,1,768]{2,1,0:T(1,128)} %compare_convert_fusion.live_ref, bf16[1536,2048]{1,0:T(8,128)(2,1)} %tok_ref.1, bf16[1536,2048]{1,0:T(8,128)(2,1)} %ups_ref.1, bf16[32,32,256]{2,1,0:T(8,128)(2,1)} %gate_ref.1, ...), custom_call_target="tpu_custom_call" | custom-call | flops 25769803776 | bytes 18874368 | tf_op jit(solution)/shard_map/expert_step/pallas_call | solution.py:525
  201.2 3.9 %to_experts.1 = (f32[32,32,256]{2,1,0:T(8,128)}, f32[32,32,256]{2,1,0:T(8,128)}, f32[32,32,256]{2,1,0:T(8,128)}) custom-call(s32[2,16]{1,0:T(2,128)} %assign_ref.3, bf16[2,16,3,32,256]{4,3,2,1,0:T(8,128)(2,1)} %get-tuple-element.10.recv_ref), custom_call_target="tpu_custom_call" | custom-call | tf_op jit(solution)/shard_map/to_experts/pallas_call | solution.py:542
  205.1 6.6 %copy.12 = bf16[1536,2048]{1,0:T(8,128)(2,1)} copy(bf16[1536,2048]{1,0:T(8,128)(2,1)} %get-tuple-element.18) | data formatting | bytes 12582912
  (1 shorter events, 0.0 us)
where the time goes:
time: 212 us
  Pallas kernels  203 us (96%)
  local copies, waits for them, and re-layouts  7.58 us (4%)
    pallas_call x1, Pallas kernels, local(): pl.pallas_call(functools.partial(fused_kernel, cfg), out_shape=(jax.Shape...  199 us
    unnamed x1, local copies, waits for them, and re-layouts  6.61 us

commit v1 on v0

--- a/solution.py
+++ b/solution.py
@@ -13,20 +13,22 @@
 NT = (((1,), (1,)), ((), ()))
 NN = (((1,), (0,)), ((), ()))
 
-NA = 9
+NB = 7
+HB = 3
 HA = 5
-HB = 3
 VMEM_BYTES = 67043328
 
 
-def fused_kernel(cfg, assign_ref, live_ref, tok_ref, ups_ref, gate_ref, up_ref, down_ref,
+def fused_kernel(cfg, assign_ref, counts_ref, tok_ref, ups_ref, gate_ref, up_ref, down_ref,
                  tg_out, recv_out,
                  stage, wfull, part, rz, rhla, rhlb, rhra, rhrb, rfla, rflb, rfra, rfrb, rza,
                  xg, acc, t3, gn, tg,
-                 w_send, w_recv, g_send, g_recv, ag_send, ag_recv, rs_send, rs_recv,
+                 w_send, w_recv_b, w_recv_a, g_send, g_recv, ag_send, ag_recv, rs_send, rs_recv,
                  xg_sem, tg_sem, own_sem):
-    G, NX, steps, block, rows, width, units = cfg
-    NB = units - NA
+    G, NX, steps, block, rows, width, batches = cfg
+    units = G
+    batch_rows = block // batches
+    NA = units - NB
     half = units // 2
     hrows = half * rows
     dp = lax.axis_index("dp")
@@ -44,22 +46,29 @@
     dev_l = {"dp": pL, "expert": g}
     dev_z = {"dp": qS, "expert": g}
 
-    A = pl.ds(0, NA)
-    A1 = pl.ds(0, HA)
-    A2 = pl.ds(HA, NA - HA)
-    B = pl.ds(NA, NB)
-    B1 = pl.ds(NA, HB)
-    B2 = pl.ds(NA + HB, NB - HB)
-
-    def peer(j):
-        gp = (g + j) % G
-        zp = (z + zh + gp // half) % 2
-        return gp, {"dp": zp * NX + x, "expert": gp}
+    B = pl.ds(0, NB)
+    B1 = pl.ds(0, HB)
+    B2 = pl.ds(HB, NB - HB)
+    A = pl.ds(NB, NA)
+    A1 = pl.ds(NB, HA)
+    A2 = pl.ds(NB + HA, NA - HA)
+
+    NY = half // 2
+    y = (g // 2) % NY
+    core = g % 2
+
+    def peer(u, sign):
+        k = (u % half) // 2
+        dy = k + (k // 2) * (5 - 2 * k)
+        far = u // half
+        yp = (y + sign * dy + NY) % NY
+        gp = ((zh + far) % 2) * half + yp * 2 + (core + u) % 2
+        return gp, {"dp": ((z + far) % 2) * NX + x, "expert": gp}
 
     barrier = pltpu.get_barrier_semaphore()
 
     def greet(j, carry):
-        pl.semaphore_signal(barrier, inc=1, device_id=peer(j)[1], device_id_type=MESH)
+        pl.semaphore_signal(barrier, inc=1, device_id=peer(j, 1)[1], device_id_type=MESH)
         return carry
 
     lax.fori_loop(1, G, greet, 0)
@@ -89,24 +98,25 @@
             return carry
 
         lax.fori_loop(0, G, one, 0)
-        wfull[s, pS, g] = stage[s, g]
+        wfull[s, pS, 0] = stage[s, g]
 
     pick(0)
     pl.semaphore_wait(barrier, G - 1 + 3)
 
     def spread(s):
-        def one(j, carry):
-            gp, dev = peer(j)
+        def one(u, carry, recv):
+            gp, dev = peer(u, -1)
             pltpu.make_async_remote_copy(
-                stage.at[s, gp], wfull.at[s, dev["dp"], g], w_send.at[s], w_recv.at[s],
+                stage.at[s, gp], wfull.at[s, dev["dp"], u], w_send.at[s], recv.at[s],
                 device_id=dev, device_id_type=MESH).start()
             return carry
 
-        lax.fori_loop(1, G, one, 0)
-
-    def spread_wait(s):
-        few = pl.ds(0, G - 1)
-        pltpu.make_async_copy(stage.at[s, few], stage.at[s, few], w_recv.at[s]).wait()
+        lax.fori_loop(1, NB, functools.partial(one, recv=w_recv_b), 0)
+        lax.fori_loop(NB, G, functools.partial(one, recv=w_recv_a), 0)
+
+    def bytes_of(count, sem):
+        some = stage.at[0, pl.ds(0, count)]
+        return pltpu.make_async_copy(some, some, sem)
 
     pending = []
 
@@ -126,13 +136,14 @@
             self.c[k] = send(ref, ref, ag_send.at[self.s, k], ag_recv.at[self.s, k], dev)
 
         def first(self):
-            spread_wait(self.s)
+            bytes_of(NB - 1, w_recv_b.at[self.s]).wait()
             self.go(0, pS, B, dev_r)
             self.go(1, pS, B, dev_l)
+            self.go(5, pS, B, dev_z)
+            bytes_of(NA, w_recv_a.at[self.s]).wait()
             self.go(2, pS, A, dev_z)
             self.go(3, pS, A, dev_r)
             self.go(4, pS, A, dev_l)
-            self.go(5, pS, B, dev_z)
 
         def w(self, *ks):
             for k in ks:
@@ -202,29 +213,24 @@
             self.go(2, pt.at[qO, B], rz.at[s, 2], dev_z)
             self.go(3, pt.at[pO, A1], rhla.at[s, 0], dev_r)
             self.go(4, pt.at[pO, A2], rhra.at[s, 0], dev_l)
-
-        def first_z(self):
-            s = self.s
-            pt = part.at[s]
             self.go(5, pt.at[qR, B], rz.at[s, 1], dev_z)
             self.go(6, pt.at[qL, B], rz.at[s, 3], dev_z)
-            self.go(7, pt.at[qS, B], rz.at[s, 0], dev_z)
 
         def mid_q(self):
             s = self.s
             pt = part.at[s]
             self.w(0)
-            add_units(HA, lambda i: pt.at[qR, i], lambda i: rhla.at[s, 1, i])
+            add_units(HA, lambda i: pt.at[qR, NB + i], lambda i: rhla.at[s, 1, i])
             self.go(8, pt.at[qR, A], rfla.at[s, 1], dev_r)
             self.w(1)
-            add_units(NA - HA, lambda i: pt.at[qL, HA + i], lambda i: rhra.at[s, 1, i])
+            add_units(NA - HA, lambda i: pt.at[qL, NB + HA + i], lambda i: rhra.at[s, 1, i])
             self.go(9, pt.at[qL, A], rfra.at[s, 1], dev_l)
 
         def opp_b(self):
             s = self.s
             pt = part.at[s]
             self.w(2)
-            add_units(NB, lambda i: pt.at[pO, NA + i], lambda i: rz.at[s, 2, i])
+            add_units(NB, lambda i: pt.at[pO, i], lambda i: rz.at[s, 2, i])
             self.go(10, pt.at[pO, B1], rhlb.at[s], dev_r)
             self.go(11, pt.at[pO, B2], rhrb.at[s], dev_l)
 
@@ -232,57 +238,66 @@
             s = self.s
             pt = part.at[s]
             self.w(3)
-            add_units(HA, lambda i: pt.at[pR, i], lambda i: rhla.at[s, 0, i])
+            add_units(HA, lambda i: pt.at[pR, NB + i], lambda i: rhla.at[s, 0, i])
             self.go(12, pt.at[pR, A], rfla.at[s, 0], dev_r)
             self.w(4)
-            add_units(NA - HA, lambda i: pt.at[pL, HA + i], lambda i: rhra.at[s, 0, i])
+            add_units(NA - HA, lambda i: pt.at[pL, NB + HA + i], lambda i: rhra.at[s, 0, i])
             self.go(13, pt.at[pL, A], rfra.at[s, 0], dev_l)
 
+        def to_partner(self):
+            s = self.s
+            pt = part.at[s]
+            self.w(8, 9)
+            add_units(NA, lambda i: pt.at[qS, NB + i], lambda i: rfla.at[s, 1, i], lambda i: rfra.at[s, 1, i])
+            self.go(16, pt.at[qS, A], rza.at[s], dev_z)
+            self.go(7, pt.at[qS, B], rz.at[s, 0], dev_z)
+
         def mid_b(self):
             s = self.s
             pt = part.at[s]
             self.w(5, 10)
-            add_units(HB, lambda i: pt.at[pR, NA + i], lambda i: rz.at[s, 1, i], lambda i: rhlb.at[s, i])
-            add_units(NB - HB, lambda i: pt.at[pR, NA + HB + i], lambda i: rz.at[s, 1, HB + i])
+            add_units(HB, lambda i: pt.at[pR, i], lambda i: rz.at[s, 1, i], lambda i: rhlb.at[s, i])
+            add_units(NB - HB, lambda i: pt.at[pR, HB + i], lambda i: rz.at[s, 1, HB + i])
             self.go(14, pt.at[pR, B], rflb.at[s], dev_r)
             self.w(6, 11)
-            add_units(HB, lambda i: pt.at[pL, NA + i], lambda i: rz.at[s, 3, i])
-            add_units(NB - HB, lambda i: pt.at[pL, NA + HB + i], lambda i: rz.at[s, 3, HB + i], lambda i: rhrb.at[s, i])
+            add_units(HB, lambda i: pt.at[pL, i], lambda i: rz.at[s, 3, i])
+            add_units(NB - HB, lambda i: pt.at[pL, HB + i], lambda i: rz.at[s, 3, HB + i], lambda i: rhrb.at[s, i])
             self.go(15, pt.at[pL, B], rfrb.at[s], dev_l)
 
-        def to_partner(self):
-            s = self.s
-            pt = part.at[s]
-            self.w(8, 9)
-            add_units(NA, lambda i: pt.at[qS, i], lambda i: rfla.at[s, 1, i], lambda i: rfra.at[s, 1, i])
-            self.go(16, pt.at[qS, A], rza.at[s], dev_z)
-
-        def finish(self):
-            s = self.s
-            pt = part.at[s]
-            self.w(7, 14, 15)
-            add_units(NB, lambda i: pt.at[pS, NA + i], lambda i: rz.at[s, 0, i], lambda i: rflb.at[s, i], lambda i: rfrb.at[s, i])
-            self.w(12, 13, 16)
-            add_units(NA, lambda i: pt.at[pS, i], lambda i: rfla.at[s, 0, i], lambda i: rfra.at[s, 0, i], lambda i: rza.at[s, i])
-
-            def one(j, carry):
-                gp, dev = peer(j)
+        def back(self, lo, hi):
+            s = self.s
+
+            def one(u, carry):
+                gp, dev = peer(u, 1)
                 pltpu.make_async_remote_copy(
-                    pt.at[pS, gp], recv_out.at[s, g], g_send.at[s], g_recv.at[s],
+                    part.at[s, pS, u], recv_out.at[s, g], g_send.at[s], g_recv.at[s],
                     device_id=dev, device_id_type=MESH).start()
                 return carry
 
-            lax.fori_loop(1, G, one, 0)
-            pltpu.make_async_copy(pt.at[pS, g], recv_out.at[s, g], own_sem.at[s]).start()
+            lax.fori_loop(lo, hi, one, 0)
+
+        def finish_a(self):
+            s = self.s
+            pt = part.at[s]
+            self.w(12, 13, 16)
+            add_units(NA, lambda i: pt.at[pS, NB + i], lambda i: rfla.at[s, 0, i], lambda i: rfra.at[s, 0, i], lambda i: rza.at[s, i])
+            self.back(NB, G)
+
+        def finish_b(self):
+            s = self.s
+            pt = part.at[s]
+            self.w(7, 14, 15)
+            add_units(NB, lambda i: pt.at[pS, i], lambda i: rz.at[s, 0, i], lambda i: rflb.at[s, i], lambda i: rfrb.at[s, i])
+            self.back(1, NB)
+            pltpu.make_async_copy(part.at[s, pS, 0], recv_out.at[s, g], own_sem.at[s]).start()
 
         def done(self):
             s = self.s
-            few = pl.ds(0, G - 1)
-            pltpu.make_async_copy(recv_out.at[s, few], recv_out.at[s, few], g_recv.at[s]).wait()
-            pltpu.make_async_copy(part.at[s, pS, 0], recv_out.at[s, 0], own_sem.at[s]).wait()
+            bytes_of(G - 1, g_recv.at[s]).wait()
+            pltpu.make_async_copy(part.at[s, pS, 0], recv_out.at[s, g], own_sem.at[s]).wait()
 
     def shard_of(p, h):
-        return ((p // NX + h + zh) % 2) * NX + p % NX
+        return ((p // NX + h) % 2) * NX + p % NX
 
     def weight(s, p, h, m):
         return wfull[s, p, pl.ds(h * half, half), m].reshape(hrows, width)
@@ -300,7 +315,10 @@
         lax.fori_loop(0, 6, one, 0)
 
     def gates(s):
-        live = live_ref[s] > 0.5
+        lane = lax.broadcasted_iota(jnp.int32, (1, block), 1)
+        live = lane < 0
+        for b in range(batches):
+            live = live | ((lane >= b * batch_rows) & (lane < b * batch_rows + counts_ref[s * batches + b]))
         tall = 32
 
         def one(j, carry):
@@ -405,7 +423,6 @@
     token_grads(0, 0, 4)
     g1.relay_pa()
     r0.first()
-    r0.first_z()
     token_grads(0, 4, 8)
     wait_xg(1)
     forward(1, pS, start=True)
@@ -427,65 +444,78 @@
     r0.mid_p()
     parts(1, qO)
     parts(1, pO)
+    r0.to_partner()
     parts(1, qR)
     parts(1, qL)
     r0.mid_b()
+    r1.first()
     parts(1, qS)
     parts(1, pR)
     parts(1, pL)
     parts(1, pS)
-    r0.to_partner()
-    r1.first()
-    r1.first_z()
-    tg_wait(0)
-    turn()
-    token_grads(1, 0, 8)
-    r0.finish()
+    r0.finish_a()
+    r0.finish_b()
     r1.mid_q()
     r1.opp_b()
     r1.mid_p()
+    tg_wait(0)
+    turn()
+    r1.to_partner()
+    token_grads(1, 0, 8)
     r1.mid_b()
-    r1.to_partner()
-    r1.finish()
+    r1.finish_a()
+    r1.finish_b()
     tg_wait(1)
-    r0.done()
-    r1.done()
     for copy in pending:
         copy.wait_send()
     for s in range(steps):
-        few = pl.ds(0, G - 1)
-        pltpu.make_async_copy(stage.at[s, few], stage.at[s, few], w_send.at[s]).wait()
-        pltpu.make_async_copy(stage.at[s, few], stage.at[s, few], g_send.at[s]).wait()
-
-
-def home_kernel(assign_ref, recv_ref, gate_ref, up_ref, down_ref):
+        bytes_of(G - 1, w_send.at[s]).wait()
+        bytes_of(G - 1, g_send.at[s]).wait()
+    r0.done()
+    r1.done()
+
+
+def home_kernel(assign_ref, recv_ref, tg_in, gate_ref, up_ref, down_ref, tg_out,
+                recv, sums, tg, recv_sem, sum_sem, in_sem, out_sem):
+    steps, count = recv.shape[:2]
+    chunks = tg.shape[0]
     outs = (gate_ref, up_ref, down_ref)
-    steps, count = recv_ref.shape[:2]
-    for ref in outs:
-        ref[...] = jnp.zeros_like(ref)
-
-    def one(i, carry):
-        s, k = i // count, i % count
-        c = assign_ref[s, k]
-        for m, ref in enumerate(outs):
-            ref[c] += recv_ref[s, k, m].astype(F32)
-        return carry
-
-    lax.fori_loop(0, steps * count, one, 0)
+    fetch = pltpu.make_async_copy(recv_ref, recv, recv_sem)
+    fetch.start()
+    tall = tg.shape[1]
+    into = [pltpu.make_async_copy(tg_in.at[pl.ds(i * tall, tall)], tg.at[i], in_sem.at[i]) for i in range(chunks)]
+    away = [pltpu.make_async_copy(tg.at[i], tg_out.at[pl.ds(i * tall, tall)], out_sem.at[i]) for i in range(chunks)]
+    for copy in into:
+        copy.start()
+    sums[...] = jnp.zeros_like(sums)
+    fetch.wait()
+    share = chunks // len(outs)
+    home = []
+    for m, ref in enumerate(outs):
+        for i in range(m * share, (m + 1) * share):
+            into[i].wait()
+            away[i].start()
+
+        def one(i, carry):
+            s, k = i // count, i % count
+            sums[m, assign_ref[s, k]] += recv[s, k, m].astype(F32)
+            return carry
+
+        lax.fori_loop(0, steps * count, one, 0)
+        home.append(pltpu.make_async_copy(sums.at[m], ref, sum_sem.at[m]))
+        home[-1].start()
+    for copy in home + away:
+        copy.wait()
 
 
 def local(tokens, upstream, counts, assign, gate_weight, up_weight, down_weight):
     steps, G = assign.shape
     batch_count = counts.shape[0] // steps
     block = tokens.shape[0] // steps
-    batch_rows = block // batch_count
     experts, rows, width = gate_weight.shape
     dp_count = tokens.shape[1] // width
     NX = dp_count // 2
-    position = jnp.arange(batch_rows, dtype=jnp.int32)
-    live = (position[None, :] < counts[:, None]).astype(F32).reshape(steps, 1, block)
-
-    NB = G - NA
+    NA = G - NB
     unit = (3, rows, width)
 
     def vm(*shape, dtype=BF16):
@@ -513,14 +543,14 @@
         vm(3, 2, hrows, block),
         vm(2, 2, block, hrows),
         vm(dp_count, block, width),
-        dma((steps,)), dma((steps,)), dma((steps,)), dma((steps,)),
+        dma((steps,)), dma((steps,)), dma((steps,)), dma((steps,)), dma((steps,)),
         dma((steps, 18)), dma((steps, 18)), dma((steps, 17)), dma((steps, 17)),
         dma((steps,)), dma((dp_count,)), dma((steps,)),
     ]
     vmem = pl.BlockSpec(memory_space=pltpu.VMEM)
     smem = pl.BlockSpec(memory_space=pltpu.SMEM)
     anyw = pl.BlockSpec(memory_space=pl.ANY)
-    cfg = (G, NX, steps, block, rows, width, G)
+    cfg = (G, NX, steps, block, rows, width, batch_count)
     flops = 2 * steps * 8 * block * (G * rows) * tokens.shape[1]
     token_grad, received = pl.pallas_call(
         functools.partial(fused_kernel, cfg),
@@ -528,7 +558,7 @@
             jax.ShapeDtypeStruct(tokens.shape, BF16),
             jax.ShapeDtypeStruct((steps, G, *unit), BF16),
         ),
-        in_specs=[smem, vmem, anyw, anyw, vmem, vmem, vmem],
+        in_specs=[smem, smem, anyw, anyw, vmem, vmem, vmem],
         out_specs=(anyw, anyw),
         scratch_shapes=scratch,
         compiler_params=pltpu.CompilerParams(
@@ -536,17 +566,24 @@
         ),
         cost_estimate=pl.CostEstimate(flops=flops, bytes_accessed=6 * tokens.size, transcendentals=0),
         name="expert_step",
-    )(assign, live, tokens, upstream, gate_weight, up_weight, down_weight)
+    )(assign, counts, tokens, upstream, gate_weight, up_weight, down_weight)
 
     grad = jax.ShapeDtypeStruct(gate_weight.shape, F32)
-    grads = pl.pallas_call(
+    chunks = 12
+    return_grads = pl.pallas_call(
         home_kernel,
-        out_shape=(grad, grad, grad),
-        in_specs=[smem, vmem],
-        out_specs=(vmem, vmem, vmem),
+        out_shape=(grad, grad, grad, jax.ShapeDtypeStruct(tokens.shape, BF16)),
+        in_specs=[smem, anyw, anyw],
+        out_specs=(anyw, anyw, anyw, anyw),
+        scratch_shapes=[
+            vm(steps, G, *unit),
+            vm(3, *gate_weight.shape, dtype=F32),
+            vm(chunks, tokens.shape[0] // chunks, tokens.shape[1]),
+            dma, dma((3,)), dma((chunks,)), dma((chunks,)),
+        ],
         name="to_experts",
-    )(assign, received)
-    return (token_grad, *grads)
+    )(assign, received, token_grad)
+    return (return_grads[3], *return_grads[:3])
 
 
 def solution(mesh):

time: 212 us -> 197 us (0.929)
  local copies, waits for them, and re-layouts: 7.58 us -> 0 us
  Pallas kernels: 203 us -> 196 us
    pallas_call x1, Pallas kernels: 199 us -> 188 us  [local(): pl.pallas_call(functools.partial(fused_kernel, cfg), out_shape=(jax.Shape...]
    unnamed x1 -> x0, local copies, waits for them, and re-layouts: 6.61 us -> none
    pallas_call x1, Pallas kernels: 3.92 us -> 7.72 us  [local(): pl.pallas_call(home_kernel, out_shape=(grad, grad, grad, jax.ShapeDtypeSt...]
where the time goes in v1:
time: 197 us
  Pallas kernels  196 us (99%)
    pallas_call x1, Pallas kernels, local(): pl.pallas_call(functools.partial(fused_kernel, cfg), out_shape=(jax.Shape...  188 us
    pallas_call x1, Pallas kernels, local(): pl.pallas_call(home_kernel, out_shape=(grad, grad, grad, jax.ShapeDtypeSt...  7.72 us

profile of v1, /device:TPU:1, one launch (start us, length us, event | category | flops | bytes accessed | tf_op | source)
XLA Modules:
  0.0 196.5 jit_solution(3464138306756748665)
XLA Ops:
  0.6 188.2 %expert_step.1 = (bf16[1536,2048]{1,0:T(8,128)(2,1)}, bf16[2,16,3,32,256]{4,3,2,1,0:T(8,128)(2,1)}) custom-call(s32[2,16]{1,0:T(2,128)} %assign_ref.3, s32[16]{0:T(128)} %counts_ref.1, bf16[1536,2048]{1,0:T(8,128)(2,1)} %tok_ref.1, bf16[1536,2048]{1,0:T(8,128)(2,1)} %ups_ref.1, bf16[32,32,256]{2,1,0:T(8,128)(2,1)} %gate_ref.1, bf16[32,32,256]{2,1,0:T(8,128)(2,1)} %up_ref.1, ...), custom_call_target="tpu_custom_call" | custom-call | flops 25769803776 | bytes 18874368 | tf_op jit(solution)/shard_map/expert_step/pallas_call | solution.py:555
  188.8 7.7 %to_experts.1 = (f32[32,32,256]{2,1,0:T(8,128)}, f32[32,32,256]{2,1,0:T(8,128)}, f32[32,32,256]{2,1,0:T(8,128)}, bf16[1536,2048]{1,0:T(8,128)(2,1)}) custom-call(s32[2,16]{1,0:T(2,128)} %assign_ref.3, bf16[2,16,3,32,256]{4,3,2,1,0:T(8,128)(2,1)} %get-tuple-element.10.recv_ref, bf16[1536,2048]{1,0:T(8,128)(2,1)} %get-tuple-element.11.tg_in), custom_call_target="tpu_custom_call" | custom-call | tf_op jit(solution)/shard_map/to_experts/pallas_call | solution.py:573

commit v2 on v1

--- a/solution.py
+++ b/solution.py
@@ -14,17 +14,18 @@
 NN = (((1,), (0,)), ((), ()))
 
 NB = 7
-HB = 3
-HA = 5
-VMEM_BYTES = 67043328
+N0 = 2
+HAS = (5, 4)
+HBS = (3, 4)
+VMEM_BYTES = 55 * 2**20
 
 
 def fused_kernel(cfg, assign_ref, counts_ref, tok_ref, ups_ref, gate_ref, up_ref, down_ref,
-                 tg_out, recv_out,
+                 tg, recv_out,
                  stage, wfull, part, rz, rhla, rhlb, rhra, rhrb, rfla, rflb, rfra, rfrb, rza,
-                 xg, acc, t3, gn, tg,
-                 w_send, w_recv_b, w_recv_a, g_send, g_recv, ag_send, ag_recv, rs_send, rs_recv,
-                 xg_sem, tg_sem, own_sem):
+                 xg, acc, t3, gn,
+                 w_send, w_recv_c, w_recv_b, w_recv_a, g_send, g_recv, ag_send, ag_recv, rs_send, rs_recv,
+                 xg_sem):
     G, NX, steps, block, rows, width, batches = cfg
     units = G
     batch_rows = block // batches
@@ -47,11 +48,13 @@
     dev_z = {"dp": qS, "expert": g}
 
     B = pl.ds(0, NB)
-    B1 = pl.ds(0, HB)
-    B2 = pl.ds(HB, NB - HB)
+    BO = pl.ds(0, N0)
+    BN = pl.ds(N0, NB - N0)
     A = pl.ds(NB, NA)
-    A1 = pl.ds(NB, HA)
-    A2 = pl.ds(NB + HA, NA - HA)
+    B1 = [pl.ds(0, h) for h in HBS]
+    B2 = [pl.ds(h, NB - h) for h in HBS]
+    A1 = [pl.ds(NB, h) for h in HAS]
+    A2 = [pl.ds(NB + h, NA - h) for h in HAS]
 
     NY = half // 2
     y = (g // 2) % NY
@@ -111,7 +114,8 @@
                 device_id=dev, device_id_type=MESH).start()
             return carry
 
-        lax.fori_loop(1, NB, functools.partial(one, recv=w_recv_b), 0)
+        lax.fori_loop(1, N0, functools.partial(one, recv=w_recv_c), 0)
+        lax.fori_loop(N0, NB, functools.partial(one, recv=w_recv_b), 0)
         lax.fori_loop(NB, G, functools.partial(one, recv=w_recv_a), 0)
 
     def bytes_of(count, sem):
@@ -136,10 +140,14 @@
             self.c[k] = send(ref, ref, ag_send.at[self.s, k], ag_recv.at[self.s, k], dev)
 
         def first(self):
-            bytes_of(NB - 1, w_recv_b.at[self.s]).wait()
-            self.go(0, pS, B, dev_r)
-            self.go(1, pS, B, dev_l)
-            self.go(5, pS, B, dev_z)
+            bytes_of(N0 - 1, w_recv_c.at[self.s]).wait()
+            self.go(0, pS, BO, dev_r)
+            self.go(1, pS, BO, dev_l)
+            self.go(5, pS, BO, dev_z)
+            bytes_of(NB - N0, w_recv_b.at[self.s]).wait()
+            self.go(18, pS, BN, dev_r)
+            self.go(19, pS, BN, dev_l)
+            self.go(20, pS, BN, dev_z)
             bytes_of(NA, w_recv_a.at[self.s]).wait()
             self.go(2, pS, A, dev_z)
             self.go(3, pS, A, dev_r)
@@ -150,11 +158,11 @@
                 self.c[k].wait_recv()
 
         def relay_b(self):
-            self.w(0)
-            self.go(6, pL, B1, dev_r)
+            self.w(0, 18)
+            self.go(6, pL, B1[self.s], dev_r)
             self.go(10, pL, B, dev_z)
-            self.w(1)
-            self.go(7, pR, B2, dev_l)
+            self.w(1, 19)
+            self.go(7, pR, B2[self.s], dev_l)
             self.go(11, pR, B, dev_z)
 
         def partner_a(self):
@@ -164,21 +172,21 @@
 
         def relay_a(self):
             self.w(3)
-            self.go(12, pL, A1, dev_r)
+            self.go(12, pL, A1[self.s], dev_r)
             self.w(4)
-            self.go(13, pR, A2, dev_l)
+            self.go(13, pR, A2[self.s], dev_l)
 
         def opp_b(self):
             self.w(6)
-            self.go(16, pO, B1, dev_z)
+            self.go(16, pO, B1[self.s], dev_z)
             self.w(7)
-            self.go(17, pO, B2, dev_z)
+            self.go(17, pO, B2[self.s], dev_z)
 
         def relay_pa(self):
             self.w(8)
-            self.go(14, qL, A1, dev_r)
+            self.go(14, qL, A1[self.s], dev_r)
             self.w(9)
-            self.go(15, qR, A2, dev_l)
+            self.go(15, qR, A2[self.s], dev_l)
 
     def add_into(dst, *others):
         total = dst[...].astype(F32)
@@ -197,6 +205,10 @@
         def __init__(self, s):
             self.s = s
             self.c = {}
+            self.pt = part.at[s]
+            self.ha, self.hb = HAS[s], HBS[s]
+            self.rha = [(rhla.at[s, k, pl.ds(0, self.ha)], rhra.at[s, k, pl.ds(0, NA - self.ha)]) for k in (0, 1)]
+            self.rhb = (rhlb.at[s, pl.ds(0, self.hb)], rhrb.at[s, pl.ds(0, NB - self.hb)])
 
         def go(self, k, src, dst, dev):
             self.c[k] = send(src, dst, rs_send.at[self.s, k], rs_recv.at[self.s, k], dev)
@@ -206,63 +218,57 @@
                 self.c[k].wait_recv()
 
         def first(self):
-            s = self.s
-            pt = part.at[s]
-            self.go(0, pt.at[qO, A1], rhla.at[s, 1], dev_r)
-            self.go(1, pt.at[qO, A2], rhra.at[s, 1], dev_l)
+            s, pt = self.s, self.pt
+            self.go(0, pt.at[qO, A1[s]], self.rha[1][0], dev_r)
+            self.go(1, pt.at[qO, A2[s]], self.rha[1][1], dev_l)
             self.go(2, pt.at[qO, B], rz.at[s, 2], dev_z)
-            self.go(3, pt.at[pO, A1], rhla.at[s, 0], dev_r)
-            self.go(4, pt.at[pO, A2], rhra.at[s, 0], dev_l)
+            self.go(3, pt.at[pO, A1[s]], self.rha[0][0], dev_r)
+            self.go(4, pt.at[pO, A2[s]], self.rha[0][1], dev_l)
             self.go(5, pt.at[qR, B], rz.at[s, 1], dev_z)
             self.go(6, pt.at[qL, B], rz.at[s, 3], dev_z)
 
+        def mid_a(self, k, near, far, row, kr, kl, into_r, into_l):
+            s, pt = self.s, self.pt
+            self.w(near)
+            add_units(self.ha, lambda i: pt.at[into_r, NB + i], lambda i: rhla.at[s, k, i])
+            self.go(kr, pt.at[into_r, A], rfla.at[s, k], dev_r)
+            self.w(far)
+            add_units(NA - self.ha, lambda i: pt.at[into_l, NB + self.ha + i], lambda i: rhra.at[s, k, i])
+            self.go(kl, pt.at[into_l, A], rfra.at[s, k], dev_l)
+
         def mid_q(self):
-            s = self.s
-            pt = part.at[s]
-            self.w(0)
-            add_units(HA, lambda i: pt.at[qR, NB + i], lambda i: rhla.at[s, 1, i])
-            self.go(8, pt.at[qR, A], rfla.at[s, 1], dev_r)
-            self.w(1)
-            add_units(NA - HA, lambda i: pt.at[qL, NB + HA + i], lambda i: rhra.at[s, 1, i])
-            self.go(9, pt.at[qL, A], rfra.at[s, 1], dev_l)
+            self.mid_a(1, 0, 1, None, 8, 9, qR, qL)
+
+        def mid_p(self):
+            self.mid_a(0, 3, 4, None, 12, 13, pR, pL)
 
         def opp_b(self):
-            s = self.s
-            pt = part.at[s]
+            s, pt = self.s, self.pt
             self.w(2)
             add_units(NB, lambda i: pt.at[pO, i], lambda i: rz.at[s, 2, i])
-            self.go(10, pt.at[pO, B1], rhlb.at[s], dev_r)
-            self.go(11, pt.at[pO, B2], rhrb.at[s], dev_l)
-
-        def mid_p(self):
-            s = self.s
-            pt = part.at[s]
-            self.w(3)
-            add_units(HA, lambda i: pt.at[pR, NB + i], lambda i: rhla.at[s, 0, i])
-            self.go(12, pt.at[pR, A], rfla.at[s, 0], dev_r)
-            self.w(4)
-            add_units(NA - HA, lambda i: pt.at[pL, NB + HA + i], lambda i: rhra.at[s, 0, i])
-            self.go(13, pt.at[pL, A], rfra.at[s, 0], dev_l)
+            self.go(10, pt.at[pO, B1[s]], self.rhb[0], dev_r)
+            self.go(11, pt.at[pO, B2[s]], self.rhb[1], dev_l)
 
         def to_partner(self):
-            s = self.s
-            pt = part.at[s]
+            s, pt = self.s, self.pt
             self.w(8, 9)
             add_units(NA, lambda i: pt.at[qS, NB + i], lambda i: rfla.at[s, 1, i], lambda i: rfra.at[s, 1, i])
             self.go(16, pt.at[qS, A], rza.at[s], dev_z)
-            self.go(7, pt.at[qS, B], rz.at[s, 0], dev_z)
+            self.go(7, pt.at[qS, BN], rz.at[s, 0, BN], dev_z)
+            self.go(17, pt.at[qS, BO], rz.at[s, 0, BO], dev_z)
 
         def mid_b(self):
-            s = self.s
-            pt = part.at[s]
+            s, pt, hb = self.s, self.pt, self.hb
             self.w(5, 10)
-            add_units(HB, lambda i: pt.at[pR, i], lambda i: rz.at[s, 1, i], lambda i: rhlb.at[s, i])
-            add_units(NB - HB, lambda i: pt.at[pR, HB + i], lambda i: rz.at[s, 1, HB + i])
-            self.go(14, pt.at[pR, B], rflb.at[s], dev_r)
+            add_units(hb, lambda i: pt.at[pR, i], lambda i: rz.at[s, 1, i], lambda i: rhlb.at[s, i])
+            add_units(NB - hb, lambda i: pt.at[pR, hb + i], lambda i: rz.at[s, 1, hb + i])
+            self.go(14, pt.at[pR, BN], rflb.at[s, BN], dev_r)
             self.w(6, 11)
-            add_units(HB, lambda i: pt.at[pL, i], lambda i: rz.at[s, 3, i])
-            add_units(NB - HB, lambda i: pt.at[pL, HB + i], lambda i: rz.at[s, 3, HB + i], lambda i: rhrb.at[s, i])
-            self.go(15, pt.at[pL, B], rfrb.at[s], dev_l)
+            add_units(hb, lambda i: pt.at[pL, i], lambda i: rz.at[s, 3, i])
+            add_units(NB - hb, lambda i: pt.at[pL, hb + i], lambda i: rz.at[s, 3, hb + i], lambda i: rhrb.at[s, i])
+            self.go(15, pt.at[pL, BN], rfrb.at[s, BN], dev_l)
+            self.go(18, pt.at[pR, BO], rflb.at[s, BO], dev_r)
+            self.go(19, pt.at[pL, BO], rfrb.at[s, BO], dev_l)
 
         def back(self, lo, hi):
             s = self.s
@@ -277,24 +283,27 @@
             lax.fori_loop(lo, hi, one, 0)
 
         def finish_a(self):
-            s = self.s
-            pt = part.at[s]
+            s, pt = self.s, self.pt
             self.w(12, 13, 16)
             add_units(NA, lambda i: pt.at[pS, NB + i], lambda i: rfla.at[s, 0, i], lambda i: rfra.at[s, 0, i], lambda i: rza.at[s, i])
             self.back(NB, G)
 
         def finish_b(self):
-            s = self.s
-            pt = part.at[s]
+            s, pt = self.s, self.pt
+
+            def total(lo, n):
+                add_units(n, lambda i: pt.at[pS, lo + i], lambda i: rz.at[s, 0, lo + i], lambda i: rflb.at[s, lo + i], lambda i: rfrb.at[s, lo + i])
+
             self.w(7, 14, 15)
-            add_units(NB, lambda i: pt.at[pS, i], lambda i: rz.at[s, 0, i], lambda i: rflb.at[s, i], lambda i: rfrb.at[s, i])
-            self.back(1, NB)
-            pltpu.make_async_copy(part.at[s, pS, 0], recv_out.at[s, g], own_sem.at[s]).start()
+            total(N0, NB - N0)
+            self.back(N0, NB)
+            self.w(17, 18, 19)
+            total(0, N0)
+            self.back(1, N0)
+            recv_out[s, g] = part[s, pS, 0]
 
         def done(self):
-            s = self.s
-            bytes_of(G - 1, g_recv.at[s]).wait()
-            pltpu.make_async_copy(part.at[s, pS, 0], recv_out.at[s, g], own_sem.at[s]).wait()
+            bytes_of(G - 1, g_recv.at[self.s]).wait()
 
     def shard_of(p, h):
         return ((p // NX + h) % 2) * NX + p % NX
@@ -354,10 +363,6 @@
 
         lax.fori_loop(0, 4, one, 0)
 
-    def tg_copy(s, d):
-        cols = pl.ds(pl.multiple_of(d * width, width), width)
-        return pltpu.make_async_copy(tg.at[d], tg_out.at[pl.ds(s * block, block), cols], tg_sem.at[d])
-
     def token_grads(s, lo, hi):
         def one(d, carry):
             total = None
@@ -365,18 +370,10 @@
                 for h in (0, 1):
                     got = jnp.dot(gn[m, h], weight(s, shard_of(d, h), h, m), preferred_element_type=F32)
                     total = got if total is None else total + got
-            tg[d] = total.astype(BF16)
-            tg_copy(s, d).start()
+            tg[s, d] = total.astype(BF16)
             return carry
 
         lax.fori_loop(lo, hi, one, 0)
-
-    def tg_wait(s):
-        def one(d, carry):
-            tg_copy(s, d).wait()
-            return carry
-
-        lax.fori_loop(0, 2 * NX, one, 0)
 
     g0, g1 = Gather(0), Gather(1)
     r0, r1 = Reduce(0), Reduce(1)
@@ -392,7 +389,7 @@
     g0.relay_a()
     forward(0, pL)
     forward(0, pR)
-    g0.w(5)
+    g0.w(5, 20)
     forward(0, qS)
     g0.opp_b()
     g0.relay_pa()
@@ -428,7 +425,7 @@
     forward(1, pS, start=True)
     forward(1, pL)
     forward(1, pR)
-    g1.w(5)
+    g1.w(5, 20)
     forward(1, qS)
     g1.w(10)
     forward(1, qL)
@@ -458,14 +455,12 @@
     r1.mid_q()
     r1.opp_b()
     r1.mid_p()
-    tg_wait(0)
     turn()
     r1.to_partner()
     token_grads(1, 0, 8)
     r1.mid_b()
     r1.finish_a()
     r1.finish_b()
-    tg_wait(1)
     for copy in pending:
         copy.wait_send()
     for s in range(steps):
@@ -475,36 +470,27 @@
     r1.done()
 
 
-def home_kernel(assign_ref, recv_ref, tg_in, gate_ref, up_ref, down_ref, tg_out,
-                recv, sums, tg, recv_sem, sum_sem, in_sem, out_sem):
+def home_kernel(assign_ref, recv, tg, gate_ref, up_ref, down_ref, tg_out, sums, sum_sem, out_sem):
     steps, count = recv.shape[:2]
-    chunks = tg.shape[0]
+    pieces, block, width = tg.shape[1:]
     outs = (gate_ref, up_ref, down_ref)
-    fetch = pltpu.make_async_copy(recv_ref, recv, recv_sem)
-    fetch.start()
-    tall = tg.shape[1]
-    into = [pltpu.make_async_copy(tg_in.at[pl.ds(i * tall, tall)], tg.at[i], in_sem.at[i]) for i in range(chunks)]
-    away = [pltpu.make_async_copy(tg.at[i], tg_out.at[pl.ds(i * tall, tall)], out_sem.at[i]) for i in range(chunks)]
-    for copy in into:
-        copy.start()
+    away = []
+    for i in range(steps * pieces):
+        s, d = i // pieces, i % pieces
+        to = tg_out.at[pl.ds(s * block, block), pl.ds(d * width, width)]
+        away.append(pltpu.make_async_copy(tg.at[s, d], to, out_sem.at[i]))
+        away[-1].start()
     sums[...] = jnp.zeros_like(sums)
-    fetch.wait()
-    share = chunks // len(outs)
-    home = []
     for m, ref in enumerate(outs):
-        for i in range(m * share, (m + 1) * share):
-            into[i].wait()
-            away[i].start()
-
         def one(i, carry):
             s, k = i // count, i % count
             sums[m, assign_ref[s, k]] += recv[s, k, m].astype(F32)
             return carry
 
         lax.fori_loop(0, steps * count, one, 0)
-        home.append(pltpu.make_async_copy(sums.at[m], ref, sum_sem.at[m]))
-        home[-1].start()
-    for copy in home + away:
+        away.append(pltpu.make_async_copy(sums.at[m], ref, sum_sem.at[m]))
+        away[-1].start()
+    for copy in away:
         copy.wait()
 
 
@@ -529,10 +515,10 @@
         vm(steps, dp_count, G, *unit),
         vm(steps, dp_count, G, *unit),
         vm(steps, 4, NB, *unit),
-        vm(steps, 2, HA, *unit),
-        vm(steps, HB, *unit),
-        vm(steps, 2, NA - HA, *unit),
-        vm(steps, NB - HB, *unit),
+        vm(steps, 2, max(HAS), *unit),
+        vm(steps, max(HBS), *unit),
+        vm(steps, 2, NA - min(HAS), *unit),
+        vm(steps, NB - min(HBS), *unit),
         vm(steps, 2, NA, *unit),
         vm(steps, NB, *unit),
         vm(steps, 2, NA, *unit),
@@ -542,10 +528,9 @@
         vm(3, 2, hrows, block, dtype=F32),
         vm(3, 2, hrows, block),
         vm(2, 2, block, hrows),
-        vm(dp_count, block, width),
-        dma((steps,)), dma((steps,)), dma((steps,)), dma((steps,)), dma((steps,)),
-        dma((steps, 18)), dma((steps, 18)), dma((steps, 17)), dma((steps, 17)),
-        dma((steps,)), dma((dp_count,)), dma((steps,)),
+        dma((steps,)), dma((steps,)), dma((steps,)), dma((steps,)), dma((steps,)), dma((steps,)),
+        dma((steps, 21)), dma((steps, 21)), dma((steps, 20)), dma((steps, 20)),
+        dma((steps,)),
     ]
     vmem = pl.BlockSpec(memory_space=pltpu.VMEM)
     smem = pl.BlockSpec(memory_space=pltpu.SMEM)
@@ -555,11 +540,11 @@
     token_grad, received = pl.pallas_call(
         functools.partial(fused_kernel, cfg),
         out_shape=(
-            jax.ShapeDtypeStruct(tokens.shape, BF16),
-            jax.ShapeDtypeStruct((steps, G, *unit), BF16),
+            pltpu.VMEM((steps, dp_count, block, width), BF16),
+            pltpu.VMEM((steps, G, *unit), BF16),
         ),
         in_specs=[smem, smem, anyw, anyw, vmem, vmem, vmem],
-        out_specs=(anyw, anyw),
+        out_specs=(vmem, vmem),
         scratch_shapes=scratch,
         compiler_params=pltpu.CompilerParams(
             collective_id=0, has_side_effects=True, vmem_limit_bytes=VMEM_BYTES
@@ -569,20 +554,19 @@
     )(assign, counts, tokens, upstream, gate_weight, up_weight, down_weight)
 
     grad = jax.ShapeDtypeStruct(gate_weight.shape, F32)
-    chunks = 12
+    in_vmem = functools.partial(pltpu.with_memory_space_constraint, memory_space=pltpu.VMEM)
     return_grads = pl.pallas_call(
         home_kernel,
         out_shape=(grad, grad, grad, jax.ShapeDtypeStruct(tokens.shape, BF16)),
-        in_specs=[smem, anyw, anyw],
+        in_specs=[smem, vmem, vmem],
         out_specs=(anyw, anyw, anyw, anyw),
         scratch_shapes=[
-            vm(steps, G, *unit),
             vm(3, *gate_weight.shape, dtype=F32),
-            vm(chunks, tokens.shape[0] // chunks, tokens.shape[1]),
-            dma, dma((3,)), dma((chunks,)), dma((chunks,)),
+            dma((3,)), dma((steps * dp_count,)),
         ],
+        compiler_params=pltpu.CompilerParams(vmem_limit_bytes=16 * 2**20),
         name="to_experts",
-    )(assign, received, token_grad)
+    )(assign, in_vmem(received), in_vmem(token_grad))
     return (return_grads[3], *return_grads[:3])
 
 

time: 197 us -> 190 us (0.964)
  Pallas kernels: 196 us -> 189 us
    pallas_call x1, Pallas kernels: 188 us -> 184 us  [local(): pl.pallas_call(functools.partial(fused_kernel, cfg), out_shape=(pltpu.VME...]
    pallas_call x1, Pallas kernels: 7.72 us -> 4.33 us  [local(): pl.pallas_call(home_kernel, out_shape=(grad, grad, grad, jax.ShapeDtypeSt...]
where the time goes in v2:
time: 190 us; the launch traced here: 189 us
  Pallas kernels  189 us (99%)
    pallas_call x1, Pallas kernels, local(): pl.pallas_call(functools.partial(fused_kernel, cfg), out_shape=(pltpu.VME...  184 us
    pallas_call x1, Pallas kernels, local(): pl.pallas_call(home_kernel, out_shape=(grad, grad, grad, jax.ShapeDtypeSt...  4.33 us

profile of v2, /device:TPU:1, one launch (start us, length us, event | category | flops | bytes accessed | tf_op | source)
XLA Modules:
  0.0 189.4 jit_solution(1697071069904404344)
XLA Ops:
  0.6 0.0 copy-start
  0.6 184.5 %expert_step.1 = (bf16[2,8,768,256]{3,2,1,0:T(8,128)(2,1)S(1)}, bf16[2,16,3,32,256]{4,3,2,1,0:T(8,128)(2,1)S(1)}) custom-call(s32[2,16]{1,0:T(2,128)} %assign_ref.3, s32[16]{0:T(128)} %counts_ref.1, bf16[1536,2048]{1,0:T(8,128)(2,1)} %tok_ref.1, bf16[1536,2048]{1,0:T(8,128)(2,1)} %ups_ref.1, bf16[32,32,256]{2,1,0:T(8,128)(2,1)} %gate_ref.1, ...), custom_call_target="tpu_custom_call" | custom-call | flops 25769803776 | bytes 18874368 | tf_op jit(solution)/shard_map/expert_step/pallas_call | solution.py:540
  185.1 0.0 copy-done
  185.1 4.3 %to_experts.1 = (f32[32,32,256]{2,1,0:T(8,128)}, f32[32,32,256]{2,1,0:T(8,128)}, f32[32,32,256]{2,1,0:T(8,128)}, bf16[1536,2048]{1,0:T(8,128)(2,1)}) custom-call(s32[2,16]{1,0:T(2,128)S(1)} %copy-done, bf16[2,16,3,32,256]{4,3,2,1,0:T(8,128)(2,1)S(1)} %get-tuple-element.10.recv, bf16[2,8,768,256]{3,2,1,0:T(8,128)(2,1)S(1)} %get-tuple-element.11.tg), custom_call_target="tpu_custom_call" | custom-call | tf_op jit(solution)/shard_map/to_experts/pallas_call | solution.py:558
Async XLA Ops:
  0.6 184.5 %copy-start = (s32[2,16]{1,0:T(2,128)S(1)}, s32[2,16]{1,0:T(2,128)}, u32[]{:S(2)}) copy-start(s32[2,16]{1,0:T(2,128)} %assign_ref.3) | copy-start | bytes 388

commit v3 on v2

--- a/solution.py
+++ b/solution.py
@@ -15,6 +15,8 @@
 
 NB = 7
 N0 = 2
+BGROUPS = (((0, 2), (2, 6), (6, 7)), ((0, 7),))
+AGROUPS = (((7, 10), (10, 16)), ((7, 16),))
 HAS = (5, 4)
 HBS = (3, 4)
 VMEM_BYTES = 55 * 2**20
@@ -24,8 +26,8 @@
                  tg, recv_out,
                  stage, wfull, part, rz, rhla, rhlb, rhra, rhrb, rfla, rflb, rfra, rfrb, rza,
                  xg, acc, t3, gn,
-                 w_send, w_recv_c, w_recv_b, w_recv_a, g_send, g_recv, ag_send, ag_recv, rs_send, rs_recv,
-                 xg_sem):
+                 w_send, w_recv, g_send, g_recv, ag_send, ag_recv, rs_send, rs_recv,
+                 xg_sem, own, own_sem):
     G, NX, steps, block, rows, width, batches = cfg
     units = G
     batch_rows = block // batches
@@ -69,6 +71,9 @@
         return gp, {"dp": ((z + far) % 2) * NX + x, "expert": gp}
 
     barrier = pltpu.get_barrier_semaphore()
+    shards = [pltpu.make_async_copy(ref, own.at[m], own_sem.at[m]) for m, ref in enumerate((gate_ref, up_ref, down_ref))]
+    for copy in shards:
+        copy.start()
 
     def greet(j, carry):
         pl.semaphore_signal(barrier, inc=1, device_id=peer(j, 1)[1], device_id_type=MESH)
@@ -90,20 +95,20 @@
     def wait_xg(s):
         pltpu.make_async_copy(xg, xg, xg_sem.at[s]).wait()
 
-    load_xg(0)
-
     def pick(s):
         def one(i, carry):
             c = assign_ref[s, i]
-            stage[s, i, 0] = gate_ref[c]
-            stage[s, i, 1] = up_ref[c]
-            stage[s, i, 2] = down_ref[c]
+            for m in range(3):
+                stage[s, i, m] = own[m, c]
             return carry
 
         lax.fori_loop(0, G, one, 0)
         wfull[s, pS, 0] = stage[s, g]
 
+    for copy in shards:
+        copy.wait()
     pick(0)
+    load_xg(0)
     pl.semaphore_wait(barrier, G - 1 + 3)
 
     def spread(s):
@@ -114,9 +119,12 @@
                 device_id=dev, device_id_type=MESH).start()
             return carry
 
-        lax.fori_loop(1, N0, functools.partial(one, recv=w_recv_c), 0)
-        lax.fori_loop(N0, NB, functools.partial(one, recv=w_recv_b), 0)
-        lax.fori_loop(NB, G, functools.partial(one, recv=w_recv_a), 0)
+        for i, (lo, hi) in enumerate(BGROUPS[s] + AGROUPS[s]):
+            lax.fori_loop(max(lo, 1), hi, functools.partial(one, recv=w_recv.at[i]), 0)
+
+    def arrived(s, i):
+        lo, hi = (BGROUPS[s] + AGROUPS[s])[i]
+        bytes_of(hi - max(lo, 1), w_recv.at[i, s]).wait()
 
     def bytes_of(count, sem):
         some = stage.at[0, pl.ds(0, count)]
@@ -136,44 +144,57 @@
             self.c = {}
 
         def go(self, k, p, piece, dev):
+            n = len(self.c)
             ref = wfull.at[self.s, p, piece]
-            self.c[k] = send(ref, ref, ag_send.at[self.s, k], ag_recv.at[self.s, k], dev)
+            self.c[k] = send(ref, ref, ag_send.at[self.s, n], ag_recv.at[self.s, n], dev)
 
         def first(self):
-            bytes_of(N0 - 1, w_recv_c.at[self.s]).wait()
-            self.go(0, pS, BO, dev_r)
-            self.go(1, pS, BO, dev_l)
-            self.go(5, pS, BO, dev_z)
-            bytes_of(NB - N0, w_recv_b.at[self.s]).wait()
-            self.go(18, pS, BN, dev_r)
-            self.go(19, pS, BN, dev_l)
-            self.go(20, pS, BN, dev_z)
-            bytes_of(NA, w_recv_a.at[self.s]).wait()
-            self.go(2, pS, A, dev_z)
-            self.go(3, pS, A, dev_r)
-            self.go(4, pS, A, dev_l)
+            s = self.s
+            count = len(BGROUPS[s])
+            for i, (lo, hi) in enumerate(BGROUPS[s]):
+                arrived(s, i)
+                for k, dev in (("br", dev_r), ("bl", dev_l), ("bz", dev_z)):
+                    self.go((k, i), pS, pl.ds(lo, hi - lo), dev)
+            for i, (lo, hi) in enumerate(AGROUPS[s]):
+                arrived(s, count + i)
+                for k, dev in (("az", dev_z), ("ar", dev_r), ("al", dev_l)):
+                    self.go((k, i), pS, pl.ds(lo, hi - lo), dev)
+
+        def first_ready(self):
+            s = self.s
+            for i in range(len(BGROUPS[s]) + len(AGROUPS[s])):
+                arrived(s, i)
+            self.go(("az", 0), pS, A, dev_z)
+            self.go(("br", 0), pS, B, dev_r)
+            self.go(("bl", 0), pS, B, dev_l)
+            self.go(("ar", 0), pS, A, dev_r)
+            self.go(("al", 0), pS, A, dev_l)
+            self.go(("bz", 0), pS, B, dev_z)
+
+        def all_of(self, kind):
+            self.w(*[k for k in self.c if isinstance(k, tuple) and k[0] == kind])
 
         def w(self, *ks):
             for k in ks:
                 self.c[k].wait_recv()
 
         def relay_b(self):
-            self.w(0, 18)
+            self.all_of("br")
             self.go(6, pL, B1[self.s], dev_r)
             self.go(10, pL, B, dev_z)
-            self.w(1, 19)
+            self.all_of("bl")
             self.go(7, pR, B2[self.s], dev_l)
             self.go(11, pR, B, dev_z)
 
         def partner_a(self):
-            self.w(2)
+            self.all_of("az")
             self.go(8, qS, A, dev_r)
             self.go(9, qS, A, dev_l)
 
         def relay_a(self):
-            self.w(3)
+            self.all_of("ar")
             self.go(12, pL, A1[self.s], dev_r)
-            self.w(4)
+            self.all_of("al")
             self.go(13, pR, A2[self.s], dev_l)
 
         def opp_b(self):
@@ -389,11 +410,11 @@
     g0.relay_a()
     forward(0, pL)
     forward(0, pR)
-    g0.w(5, 20)
+    g0.all_of("bz")
     forward(0, qS)
     g0.opp_b()
     g0.relay_pa()
-    g1.first()
+    g1.first_ready()
     g0.w(10)
     forward(0, qL)
     g0.w(11)
@@ -425,7 +446,7 @@
     forward(1, pS, start=True)
     forward(1, pL)
     forward(1, pR)
-    g1.w(5, 20)
+    g1.all_of("bz")
     forward(1, qS)
     g1.w(10)
     forward(1, qL)
@@ -487,7 +508,7 @@
             sums[m, assign_ref[s, k]] += recv[s, k, m].astype(F32)
             return carry
 
-        lax.fori_loop(0, steps * count, one, 0)
+        lax.fori_loop(0, steps * count, one, 0, unroll=4)
         away.append(pltpu.make_async_copy(sums.at[m], ref, sum_sem.at[m]))
         away[-1].start()
     for copy in away:
@@ -528,9 +549,10 @@
         vm(3, 2, hrows, block, dtype=F32),
         vm(3, 2, hrows, block),
         vm(2, 2, block, hrows),
-        dma((steps,)), dma((steps,)), dma((steps,)), dma((steps,)), dma((steps,)), dma((steps,)),
-        dma((steps, 21)), dma((steps, 21)), dma((steps, 20)), dma((steps, 20)),
+        dma((steps,)), dma((5, steps)), dma((steps,)), dma((steps,)),
+        dma((steps, 27)), dma((steps, 27)), dma((steps, 20)), dma((steps, 20)),
         dma((steps,)),
+        vm(3, *gate_weight.shape), dma((3,)),
     ]
     vmem = pl.BlockSpec(memory_space=pltpu.VMEM)
     smem = pl.BlockSpec(memory_space=pltpu.SMEM)
@@ -543,7 +565,7 @@
             pltpu.VMEM((steps, dp_count, block, width), BF16),
             pltpu.VMEM((steps, G, *unit), BF16),
         ),
-        in_specs=[smem, smem, anyw, anyw, vmem, vmem, vmem],
+        in_specs=[smem, smem, anyw, anyw, anyw, anyw, anyw],
         out_specs=(vmem, vmem),
         scratch_shapes=scratch,
         compiler_params=pltpu.CompilerParams(

time: 190 us -> 186 us (0.979)
  Pallas kernels: 189 us -> 184 us
    pallas_call x1, Pallas kernels: 184 us -> 180 us  [local(): pl.pallas_call(functools.partial(fused_kernel, cfg), out_shape=(pltpu.VME...]
where the time goes in v3:
time: 186 us; the launch traced here: 185 us
  Pallas kernels  184 us (99%)
    pallas_call x1, Pallas kernels, local(): pl.pallas_call(functools.partial(fused_kernel, cfg), out_shape=(pltpu.VME...  180 us
    pallas_call x1, Pallas kernels, local(): pl.pallas_call(home_kernel, out_shape=(grad, grad, grad, jax.ShapeDtypeSt...  4.33 us

profile of v3, /device:TPU:1, one launch (start us, length us, event | category | flops | bytes accessed | tf_op | source)
XLA Modules:
  0.0 185.0 jit_solution(622415959690870698)
XLA Ops:
  0.6 0.0 copy-start
  0.6 180.0 %expert_step.1 = (bf16[2,8,768,256]{3,2,1,0:T(8,128)(2,1)S(1)}, bf16[2,16,3,32,256]{4,3,2,1,0:T(8,128)(2,1)S(1)}) custom-call(s32[2,16]{1,0:T(2,128)} %assign_ref.3, s32[16]{0:T(128)} %counts_ref.1, bf16[1536,2048]{1,0:T(8,128)(2,1)} %tok_ref.1, bf16[1536,2048]{1,0:T(8,128)(2,1)} %ups_ref.1, bf16[32,32,256]{2,1,0:T(8,128)(2,1)} %gate_ref.1, ...), custom_call_target="tpu_custom_call" | custom-call | flops 25769803776 | bytes 18874368 | tf_op jit(solution)/shard_map/expert_step/pallas_call | solution.py:562
  180.7 0.0 copy-done
  180.7 4.3 %to_experts.1 = (f32[32,32,256]{2,1,0:T(8,128)}, f32[32,32,256]{2,1,0:T(8,128)}, f32[32,32,256]{2,1,0:T(8,128)}, bf16[1536,2048]{1,0:T(8,128)(2,1)}) custom-call(s32[2,16]{1,0:T(2,128)S(1)} %copy-done, bf16[2,16,3,32,256]{4,3,2,1,0:T(8,128)(2,1)S(1)} %get-tuple-element.10.recv, bf16[2,8,768,256]{3,2,1,0:T(8,128)(2,1)S(1)} %get-tuple-element.11.tg), custom_call_target="tpu_custom_call" | custom-call | tf_op jit(solution)/shard_map/to_experts/pallas_call | solution.py:580
Async XLA Ops:
  0.6 180.1 %copy-start = (s32[2,16]{1,0:T(2,128)S(1)}, s32[2,16]{1,0:T(2,128)}, u32[]{:S(2)}) copy-start(s32[2,16]{1,0:T(2,128)} %assign_ref.3) | copy-start | bytes 388

commit v4 on v3

--- a/solution.py
+++ b/solution.py
@@ -400,8 +400,8 @@
     r0, r1 = Reduce(0), Reduce(1)
 
     spread(0)
+    g0.first()
     pick(1)
-    g0.first()
     spread(1)
     wait_xg(0)
     forward(0, pS, start=True)
@@ -438,16 +438,14 @@
     load_xg(1)
     g1.opp_b()
     turn()
-    token_grads(0, 0, 4)
-    g1.relay_pa()
-    r0.first()
-    token_grads(0, 4, 8)
     wait_xg(1)
     forward(1, pS, start=True)
     forward(1, pL)
     forward(1, pR)
     g1.all_of("bz")
     forward(1, qS)
+    g1.relay_pa()
+    r0.first()
     g1.w(10)
     forward(1, qL)
     g1.w(11)
@@ -462,6 +460,7 @@
     r0.mid_p()
     parts(1, qO)
     parts(1, pO)
+    token_grads(0, 0, 4)
     r0.to_partner()
     parts(1, qR)
     parts(1, qL)
@@ -471,6 +470,7 @@
     parts(1, pR)
     parts(1, pL)
     parts(1, pS)
+    token_grads(0, 4, 8)
     r0.finish_a()
     r0.finish_b()
     r1.mid_q()

time: 186 us -> 184 us (0.989)
  no operation moved by 1% of the time
where the time goes in v4:
time: 184 us
  Pallas kernels  184 us (100%)
    pallas_call x1, Pallas kernels, local(): pl.pallas_call(functools.partial(fused_kernel, cfg), out_shape=(pltpu.VME...  179 us
    pallas_call x1, Pallas kernels, local(): pl.pallas_call(home_kernel, out_shape=(grad, grad, grad, jax.ShapeDtypeSt...  4.33 us

profile of v4, /device:TPU:1, one launch (start us, length us, event | category | flops | bytes accessed | tf_op | source)
XLA Modules:
  0.0 184.2 jit_solution(10218508395509721810)
XLA Ops:
  0.6 0.0 copy-start
  0.6 179.2 %expert_step.1 = (bf16[2,8,768,256]{3,2,1,0:T(8,128)(2,1)S(1)}, bf16[2,16,3,32,256]{4,3,2,1,0:T(8,128)(2,1)S(1)}) custom-call(s32[2,16]{1,0:T(2,128)} %assign_ref.3, s32[16]{0:T(128)} %counts_ref.1, bf16[1536,2048]{1,0:T(8,128)(2,1)} %tok_ref.1, bf16[1536,2048]{1,0:T(8,128)(2,1)} %ups_ref.1, bf16[32,32,256]{2,1,0:T(8,128)(2,1)} %gate_ref.1, ...), custom_call_target="tpu_custom_call" | custom-call | flops 25769803776 | bytes 18874368 | tf_op jit(solution)/shard_map/expert_step/pallas_call | solution.py:562
  179.9 0.0 copy-done
  179.9 4.3 %to_experts.1 = (f32[32,32,256]{2,1,0:T(8,128)}, f32[32,32,256]{2,1,0:T(8,128)}, f32[32,32,256]{2,1,0:T(8,128)}, bf16[1536,2048]{1,0:T(8,128)(2,1)}) custom-call(s32[2,16]{1,0:T(2,128)S(1)} %copy-done, bf16[2,16,3,32,256]{4,3,2,1,0:T(8,128)(2,1)S(1)} %get-tuple-element.10.recv, bf16[2,8,768,256]{3,2,1,0:T(8,128)(2,1)S(1)} %get-tuple-element.11.tg), custom_call_target="tpu_custom_call" | custom-call | tf_op jit(solution)/shard_map/to_experts/pallas_call | solution.py:580
Async XLA Ops:
  0.6 179.2 %copy-start = (s32[2,16]{1,0:T(2,128)S(1)}, s32[2,16]{1,0:T(2,128)}, u32[]{:S(2)}) copy-start(s32[2,16]{1,0:T(2,128)} %assign_ref.3) | copy-start | bytes 388
